TPU v7x, 32 devices: a whole 2x2x4 slice. The times are simulated.
32 devices in a mesh: rep: 2 (over x), fsdp: 2 (over core), seq: 8 (over z, y).
Axes of the slice: x: 2, y: 2, z: 4, core: 2. Of those that a mesh axis runs over, the one named last changes fastest.
Arguments:
- tokens: bfloat16 [2, 4, 2048, 768], P(None, ('rep', 'fsdp'), 'seq'), may hold values from -6 to 6
- lengths: int32 [2, 4, 8], P(None, ('rep', 'fsdp')), may hold values from 1 to 1024, 2048 in all within a row
- ln1_gain: bfloat16 [768], P('fsdp'), may hold values from 0.099609375 to 1.8984375
- ln1_bias: bfloat16 [768], P('fsdp'), may hold values from -3 to 3
- qkv_weight: bfloat16 [768, 2304], P('fsdp'), may hold values from -0.21875 to 0.21875
- q_gain: bfloat16 [64], P('fsdp'), may hold values from 0.099609375 to 1.8984375
- k_gain: bfloat16 [64], P('fsdp'), may hold values from 0.099609375 to 1.8984375
- out_weight: bfloat16 [768, 768], P('fsdp'), may hold values from -1.75 to 1.75
- ln2_gain: bfloat16 [768], P('fsdp'), may hold values from 0.099609375 to 1.8984375
- ln2_bias: bfloat16 [768], P('fsdp'), may hold values from -3 to 3
- up_weight: bfloat16 [768, 3072], P('fsdp'), may hold values from -0.21875 to 0.21875
- down_weight: bfloat16 [3072, 768], P('fsdp'), may hold values from -0.109375 to 0.109375
- cotangent: bfloat16 [2, 4, 2048, 768], P(None, ('rep', 'fsdp'), 'seq'), may hold values from -6 to 6
Outputs:
- output: bfloat16 [2, 4, 2048, 768], P(None, ('rep', 'fsdp'), 'seq')
- grad_tokens: float32 [2, 4, 2048, 768], P(None, ('rep', 'fsdp'), 'seq')
- grad_ln1_gain: float32 [768], P('fsdp')
- grad_ln1_bias: float32 [768], P('fsdp')
- grad_qkv_weight: float32 [768, 2304], P('fsdp')
- grad_q_gain: float32 [64], P('fsdp')
- grad_k_gain: float32 [64], P('fsdp')
- grad_out_weight: float32 [768, 768], P('fsdp')
- grad_ln2_gain: float32 [768], P('fsdp')
- grad_ln2_bias: float32 [768], P('fsdp')
- grad_up_weight: float32 [768, 3072], P('fsdp')
- grad_down_weight: float32 [3072, 768], P('fsdp')
Inputs may be any that keep to these rules, and one draw needn't show every extreme that they name: In each row the first 7 entries are the lengths of its pictures in order and the last one is the padding at the row's end; each row's entries sum to 2048, and each row's largest entry is 1024.
All inputs are finite; a program needn't handle non-finite values.
Results may differ from a plain program's by a relative error of at most 0.014.
Values may be sent and summed in bfloat16 or wider, within the bound.
No kernel may reach another device: no remote copies, remote signals or barrier semaphores. Data moves between devices by JAX's collectives and lax.ppermute only.
A program may use at most 320 MiB of HBM per device.

v0:
```python
from functools import partial
import jax
import jax.numpy as jnp
from jax import lax
from jax.sharding import PartitionSpec as P

H = 12
EPS = 1e-06
MASKED = -1000000000.0


def layer_norm(values, gain, shift):
    center = jnp.mean(values, axis=-1, keepdims=True)
    centred = values - center
    spread = jnp.mean(centred * centred, axis=-1, keepdims=True)
    return centred * lax.rsqrt(spread + EPS) * gain + shift


def head_norm(values, gain):
    return layer_norm(values, gain, 0.0)


def gelu_exact(values):
    return jax.nn.gelu(values, approximate=False)


def picture_ids(lengths, length):
    bounds = jnp.cumsum(lengths, axis=-1)
    places = jnp.arange(length, dtype=jnp.int32)
    ident = jnp.sum((places[:, None] >= bounds[..., None, :-1]).astype(jnp.int32), axis=-1)
    return jnp.where(ident == lengths.shape[-1] - 1, -1, ident)


def split_groups(tensor):
    rows, length, width = tensor.shape
    shaped = tensor.reshape(rows, length, H // 2, 2, width // H)
    return jnp.moveaxis(shaped, 2, 0)


def join_groups(tensor):
    moved = jnp.moveaxis(tensor, 0, 2)
    return moved.reshape(moved.shape[0], moved.shape[1], -1)


def group_scores(q_group, k_group, same, scale):
    scores = (
        jnp.einsum("rqhd,rkhd->rhqk", q_group, k_group, preferred_element_type=jnp.float32) * scale
    )
    return jnp.where(same[:, None], scores, MASKED)


def attend_group(inputs, same, scale):
    q_group, k_group, v_group = inputs
    scores = group_scores(q_group, k_group, same, scale)
    top = jnp.max(scores, axis=-1, keepdims=True)
    expo = jnp.exp(scores - top)
    total = jnp.sum(expo, axis=-1, keepdims=True)
    probs = (expo / total).astype(jnp.bfloat16)
    context = jnp.einsum("rhqk,rkhd->rqhd", probs, v_group, preferred_element_type=jnp.float32)
    return (context, top[..., 0] + jnp.log(total[..., 0]))


def attend_back(inputs, same, scale):
    q_group, k_group, v_group, grad_group, logsum = inputs
    scores = group_scores(q_group, k_group, same, scale)
    probs = jnp.exp(scores - logsum[..., None])
    grad_probs = jnp.einsum(
        "rqhd,rkhd->rhqk", grad_group, v_group, preferred_element_type=jnp.float32
    )
    inner = jnp.sum(probs * grad_probs, axis=-1, keepdims=True)
    grad_scores = (probs * (grad_probs - inner)).astype(jnp.bfloat16)
    grad_q = (
        jnp.einsum("rhqk,rkhd->rqhd", grad_scores, k_group, preferred_element_type=jnp.float32)
        * scale
    )
    grad_k = (
        jnp.einsum("rhqk,rqhd->rkhd", grad_scores, q_group, preferred_element_type=jnp.float32)
        * scale
    )
    grad_v = jnp.einsum(
        "rhqk,rqhd->rkhd",
        probs.astype(jnp.bfloat16),
        grad_group,
        preferred_element_type=jnp.float32,
    )
    return (grad_q, grad_k, grad_v)


def unpack(weights):
    return tuple((member.astype(jnp.float32) if member.ndim == 1 else member for member in weights))


def on_device(
    tokens,
    lengths,
    ln1_gain,
    ln1_bias,
    qkv_weight,
    q_gain,
    k_gain,
    out_weight,
    ln2_gain,
    ln2_bias,
    up_weight,
    down_weight,
    cotangent,
):
    shards = (
        ln1_gain,
        ln1_bias,
        qkv_weight,
        q_gain,
        k_gain,
        out_weight,
        ln2_gain,
        ln2_bias,
        up_weight,
        down_weight,
    )
    micro, rows, local, width = tokens.shape
    head_dim = width // H
    scale = head_dim ** (-0.5)
    length = local * lax.axis_size("seq")
    offset = lax.axis_index("seq") * local

    def fetch():
        return unpack(
            (
                lax.all_gather(shards[0], "fsdp", axis=0, tiled=True),
                lax.all_gather(shards[1], "fsdp", axis=0, tiled=True),
                lax.all_gather(shards[2], "fsdp", axis=0, tiled=True),
                lax.all_gather(shards[3], "fsdp", axis=0, tiled=True),
                lax.all_gather(shards[4], "fsdp", axis=0, tiled=True),
                lax.all_gather(shards[5], "fsdp", axis=0, tiled=True),
                lax.all_gather(shards[6], "fsdp", axis=0, tiled=True),
                lax.all_gather(shards[7], "fsdp", axis=0, tiled=True),
                lax.all_gather(shards[8], "fsdp", axis=0, tiled=True),
                lax.all_gather(shards[9], "fsdp", axis=0, tiled=True),
            )
        )

    outputs = []
    grad_inputs = []
    running = None
    for index in range(micro):
        gathered = fetch()
        g_one, b_one, w_qkv, g_query, g_key, w_out, g_two, b_two, w_up, w_down = gathered
        x_block = tokens[index].astype(jnp.float32)
        ident = picture_ids(lengths[index], length)
        ident_local = lax.dynamic_slice_in_dim(ident, offset, local, 1)
        same = (ident_local[:, :, None] == ident[:, None, :]) & (ident[:, None, :] >= 0)
        valid = (ident_local >= 0).astype(jnp.float32)[..., None]
        norm_one, pull_one = jax.vjp(layer_norm, x_block, g_one, b_one)
        first = norm_one.astype(jnp.bfloat16)
        qkv = jnp.dot(first, w_qkv, preferred_element_type=jnp.float32)
        q_raw = qkv[..., :width].reshape(rows, local, H, head_dim)
        k_raw = qkv[..., width : 2 * width].reshape(rows, local, H, head_dim)
        q_normed, pull_query = jax.vjp(head_norm, q_raw, g_query)
        k_normed, pull_key = jax.vjp(head_norm, k_raw, g_key)
        queries = q_normed.astype(jnp.bfloat16).reshape(rows, local, width)
        keys = k_normed.astype(jnp.bfloat16).reshape(rows, local, width)
        values = qkv[..., 2 * width :].astype(jnp.bfloat16)
        keys_all, values_all = (
            lax.all_gather(keys, "seq", axis=1, tiled=True),
            lax.all_gather(values, "seq", axis=1, tiled=True),
        )
        q_groups = split_groups(queries)
        k_groups = split_groups(keys_all)
        v_groups = split_groups(values_all)
        context, logsum = lax.map(
            partial(attend_group, same=same, scale=scale), (q_groups, k_groups, v_groups)
        )
        attn = (join_groups(context) * valid).astype(jnp.bfloat16)
        middle = x_block + jnp.dot(attn, w_out, preferred_element_type=jnp.float32)
        norm_two, pull_two = jax.vjp(layer_norm, middle, g_two, b_two)
        second = norm_two.astype(jnp.bfloat16)
        upper = jnp.dot(second, w_up, preferred_element_type=jnp.float32)
        active_full, pull_active = jax.vjp(gelu_exact, upper)
        active = active_full.astype(jnp.bfloat16)
        result = middle + jnp.dot(active, w_down, preferred_element_type=jnp.float32)
        outputs.append(result.astype(jnp.bfloat16))
        again = fetch()
        w_qkv, w_out, w_up, w_down = (again[2], again[5], again[8], again[9])
        grad_y = cotangent[index]
        grad_down = jnp.einsum("rsf,rsd->fd", active, grad_y, preferred_element_type=jnp.float32)
        grad_active = jnp.einsum("rsd,fd->rsf", grad_y, w_down, preferred_element_type=jnp.float32)
        (grad_upper,) = pull_active(grad_active)
        grad_upper = grad_upper.astype(jnp.bfloat16)
        grad_up = jnp.einsum("rsd,rsf->df", second, grad_upper, preferred_element_type=jnp.float32)
        grad_second = jnp.einsum(
            "rsf,df->rsd", grad_upper, w_up, preferred_element_type=jnp.float32
        )
        grad_mid_norm, grad_g_two, grad_b_two = pull_two(grad_second)
        grad_middle = grad_y.astype(jnp.float32) + grad_mid_norm
        grad_branch = grad_middle.astype(jnp.bfloat16)
        grad_out = jnp.einsum("rsd,rse->de", attn, grad_branch, preferred_element_type=jnp.float32)
        grad_attn = (
            jnp.einsum("rse,de->rsd", grad_branch, w_out, preferred_element_type=jnp.float32)
            * valid
        ).astype(jnp.bfloat16)
        grad_qg, grad_kg, grad_vg = lax.map(
            partial(attend_back, same=same, scale=scale),
            (q_groups, k_groups, v_groups, split_groups(grad_attn), logsum),
        )
        grad_keys, grad_values = (
            lax.psum_scatter(
                join_groups(grad_kg).astype(jnp.bfloat16), "seq", scatter_dimension=1, tiled=True
            ).astype(jnp.float32),
            lax.psum_scatter(
                join_groups(grad_vg).astype(jnp.bfloat16), "seq", scatter_dimension=1, tiled=True
            ).astype(jnp.float32),
        )
        grad_q_raw, grad_g_query = pull_query(
            join_groups(grad_qg).reshape(rows, local, H, head_dim)
        )
        grad_k_raw, grad_g_key = pull_key(grad_keys.reshape(rows, local, H, head_dim))
        grad_qkv = jnp.concatenate(
            [
                grad_q_raw.reshape(rows, local, width),
                grad_k_raw.reshape(rows, local, width),
                grad_values,
            ],
            axis=-1,
        ).astype(jnp.bfloat16)
        grad_qkv_w = jnp.einsum("rsd,rse->de", first, grad_qkv, preferred_element_type=jnp.float32)
        grad_first = jnp.einsum("rse,de->rsd", grad_qkv, w_qkv, preferred_element_type=jnp.float32)
        grad_x_norm, grad_g_one, grad_b_one = pull_one(grad_first)
        grad_inputs.append(grad_middle + grad_x_norm)
        grads = (
            grad_g_one,
            grad_b_one,
            grad_qkv_w,
            grad_g_query,
            grad_g_key,
            grad_out,
            grad_g_two,
            grad_b_two,
            grad_up,
            grad_down,
        )
        running = grads if index == 0 else jax.tree.map(jnp.add, running, grads)
    owned = lax.psum_scatter(running, "fsdp", scatter_dimension=0, tiled=True)
    running = lax.psum(owned, ("rep", "seq"))
    output = jnp.stack(outputs, axis=0)
    grad_tokens = jnp.stack(grad_inputs, axis=0)
    return (
        output,
        grad_tokens,
        running[0],
        running[1],
        running[2],
        running[3],
        running[4],
        running[5],
        running[6],
        running[7],
        running[8],
        running[9],
    )


def solution(mesh):
    in_specs = (
        P(None, ("rep", "fsdp"), "seq", None),
        P(None, ("rep", "fsdp"), None),
        P("fsdp"),
        P("fsdp"),
        P("fsdp", None),
        P("fsdp"),
        P("fsdp"),
        P("fsdp", None),
        P("fsdp"),
        P("fsdp"),
        P("fsdp", None),
        P("fsdp", None),
        P(None, ("rep", "fsdp"), "seq", None),
    )
    out_specs = (
        P(None, ("rep", "fsdp"), "seq", None),
        P(None, ("rep", "fsdp"), "seq", None),
        P("fsdp"),
        P("fsdp"),
        P("fsdp", None),
        P("fsdp"),
        P("fsdp"),
        P("fsdp", None),
        P("fsdp"),
        P("fsdp"),
        P("fsdp", None),
        P("fsdp", None),
    )
    return jax.shard_map(
        on_device, mesh=mesh, in_specs=in_specs, out_specs=out_specs, check_vma=False
    )
```

profile of v0, /device:TPU:0, one launch (start us, length us, event | category | flops | bytes accessed | tf_op | source)
XLA Modules:
  0.0 1268.5 jit_solution(4192007691853410526)
XLA Ops:
  15.5 9.5 all-gather.13.cloned.1.call-done
  67.0 23.4 %all-gather.25.cloned.1.call-done = bf16[1,2048,768]{2,1,0:T(8,128)(2,1)} async-done(((bf16[1,256,768]{2,1,0:T(8,128)(2,1)}), bf16[1,2048,768]{2,1,0:T(8,128)(2,1)}) %all-gather.25.cloned.1.call-update) | async-done | bytes 3145744 | tf_op jit(solution)/shard_map/all_gather | solution.py:165
  90.4 4.8 copy.197
  95.3 56.6 %all-gather.27.cloned.1.call-done = bf16[1,2048,768]{2,1,0:T(8,128)(2,1)} async-done(((bf16[1,256,768]{2,1,0:T(8,128)(2,1)}), bf16[1,2048,768]{2,1,0:T(8,128)(2,1)}) %all-gather.27.cloned.1.call-update) | async-done | bytes 3145744 | tf_op jit(solution)/shard_map/all_gather | solution.py:164
  156.6 47.0 %while.57 = (s32[]{:T(128)}, f32[6,1,256,2,64]{2,4,3,1,0:T(8,128)}, f32[6,1,2,256]{3,2,1,0:T(2,128)}, bf16[6,1,2048,2,64]{2,4,3,1,0:T(8,128)(2,1)}, bf16[6,1,256...) while((s32[]{:T(128)}, f32[6,1,256,2,64]{2,4,3,1,0:T(8,128)}, ...), condition=%wide.region_25.26_spmd.clone, body=%wide.region_22.25_spmd.clone.sunk | while | flops 282066432 | bytes 15955057 | solution.py:170
  211.0 13.5 %all-gather.15.cloned.1.call-done = bf16[1,2048,768]{2,1,0:T(8,128)(2,1)} async-done(((bf16[1,256,768]{2,1,0:T(8,128)(2,1)}), bf16[1,2048,768]{2,1,0:T(8,128)(2,1)}) %all-gather.15.cloned.1.call-update) | async-done | bytes 3145744 | tf_op jit(solution)/shard_map/all_gather | solution.py:165
  224.5 4.7 copy.183
  229.2 56.7 %all-gather.17.cloned.1.call-done = bf16[1,2048,768]{2,1,0:T(8,128)(2,1)} async-done(((bf16[1,256,768]{2,1,0:T(8,128)(2,1)}), bf16[1,2048,768]{2,1,0:T(8,128)(2,1)}) %all-gather.17.cloned.1.call-update) | async-done | bytes 3145744 | tf_op jit(solution)/shard_map/all_gather | solution.py:164
  290.6 42.0 %while.56 = (s32[]{:T(128)}, f32[6,1,256,2,64]{2,4,3,1,0:T(8,128)}, f32[6,1,2,256]{3,2,1,0:T(2,128)}, bf16[6,1,2048,2,64]{2,4,3,1,0:T(8,128)(2,1)}, bf16[6,1,256...) while((s32[]{:T(128)}, f32[6,1,256,2,64]{2,4,3,1,0:T(8,128)}, ...), condition=%wide.region_11.12_spmd.clone, body=%wide.region_8.11_spmd.clone.sunk | while | flops 282066432 | bytes 15955057 | solution.py:170
  339.4 12.3 multiply_convert_fusion.2
  351.7 11.5 multiply_convert_fusion.3
  363.3 6.4 add_convert_fusion
  388.8 77.8 %while.59 = (s32[]{:T(128)}, f32[6,1,256,2,64]{2,4,3,1,0:T(8,128)}, bf16[6,1,2048,2,64]{2,4,3,1,0:T(8,128)(2,1)}, bf16[6,1,2048,2,64]{2,4,3,1,0:T(8,128)(2,1)}, ...) while((s32[]{:T(128)}, f32[6,1,256,2,64]{2,4,3,1,0:T(8,128)}, ...), condition=%wide.region_45.46_spmd.clone, body=%wide.region_43.45_spmd.clone.sunk | while | flops 681868800 | bytes 36608192 | solution.py:201
  466.6 4.7 copy.242
  481.6 59.9 %while.58 = (s32[]{:T(128)}, f32[6,1,256,2,64]{2,4,3,1,0:T(8,128)}, bf16[6,1,2048,2,64]{2,4,3,1,0:T(8,128)(2,1)}, bf16[6,1,2048,2,64]{2,4,3,1,0:T(8,128)(2,1)}, ...) while((s32[]{:T(128)}, f32[6,1,256,2,64]{2,4,3,1,0:T(8,128)}, ...), condition=%wide.region_32.33_spmd.clone, body=%wide.region_30.32_spmd.clone.sunk | while | flops 681868800 | bytes 36595848 | solution.py:201
  541.5 4.7 copy.223
  562.8 5.3 convolution_add_fusion.2
  572.3 5.2 convolution_add_fusion.1
  600.6 20.7 %reduce-scatter.9.cloned.1.call-done = bf16[1,256,768]{2,1,0:T(8,128)(2,1)} async-done(((bf16[1,2048,768]{2,1,0:T(8,128)(2,1)}), bf16[1,256,768]{2,1,0:T(8,128)(2,1)}) %reduce-scatter.9.cloned.1.call-update) | async-done | bytes 393232 | tf_op jit(solution)/shard_map/reduce_scatter | solution.py:206
  631.7 5.1 multiply_reduce_fusion.5
  636.7 62.2 %reduce-scatter.11.cloned.1.call-done = bf16[1,256,768]{2,1,0:T(8,128)(2,1)} async-done(((bf16[1,2048,768]{2,1,0:T(8,128)(2,1)}), bf16[1,256,768]{2,1,0:T(8,128)(2,1)}) %reduce-scatter.11.cloned.1.call-update) | async-done | bytes 393232 | tf_op jit(solution)/shard_map/reduce_scatter | solution.py:209
  699.0 5.5 fusion.159
  707.1 69.6 %reduce-scatter.15.cloned.1.call-done = bf16[1,256,768]{2,1,0:T(8,128)(2,1)} async-done(((bf16[1,2048,768]{2,1,0:T(8,128)(2,1)}), bf16[1,256,768]{2,1,0:T(8,128)(2,1)}) %reduce-scatter.15.cloned.1.call-update) | async-done | bytes 393232 | tf_op jit(solution)/shard_map/reduce_scatter | solution.py:209
  776.7 7.4 convolution_add_fusion
  784.5 4.3 reduce-scatter.19.cloned.1.call-done
  788.8 20.7 %reduce-scatter.21.cloned.1.call-done = f32[384,3072]{1,0:T(8,128)} async-done(((f32[768,3072]{1,0:T(8,128)}), f32[384,3072]{1,0:T(8,128)}) %reduce-scatter.21.cloned.1.call-update) | async-done | bytes 4718608 | tf_op jit(solution)/shard_map/reduce_scatter | solution.py:242
  809.5 20.7 %reduce-scatter.23.cloned.1.call-done = f32[1536,768]{1,0:T(8,128)} async-done(((f32[3072,768]{1,0:T(8,128)}), f32[1536,768]{1,0:T(8,128)}) %reduce-scatter.23.cloned.1.call-update) | async-done | bytes 4718608 | tf_op jit(solution)/shard_map/reduce_scatter | solution.py:242
  830.2 19.3 %reduce-scatter.17.cloned.1.call-done = f32[384,2304]{1,0:T(8,128)} async-done(((f32[768,2304]{1,0:T(8,128)}), f32[384,2304]{1,0:T(8,128)}) %reduce-scatter.17.cloned.1.call-update) | async-done | bytes 3538960 | tf_op jit(solution)/shard_map/reduce_scatter | solution.py:242
  852.6 4.3 fusion.110
  870.3 4.2 all-reduce.10
  874.9 47.1 %all-reduce.8 = (f32[384]{0:T(512)}, f32[384]{0:T(512)}, f32[32]{0:T(128)}, f32[32]{0:T(128)}, f32[384]{0:T(512)}, /*index=5*/f32[384]{0:T(512)}) all-reduce(f32[384]{0:T(512)S(1)} %dynamic-slice.3, f32[384]{0:T(512)S(1)} %dynamic-slice.5, f32[32]{0:T(128)S(1)} %dynamic-slice.7, ...), channel_id=1, replica_groups=mesh['rep'=2,'fsdp'=2,'seq'=8] {'rep','seq'}, use_global_device_ids=true, to_apply=%region_57.58 | all-reduce | flops 1600 | bytes 12800 | tf_op jit(solution)/shard_map/psum | solution.py:243
  925.4 325.2 %all-reduce.14.cloned.1.call-done = (f32[384,2304]{1,0:T(8,128)}, f32[384,768]{1,0:T(8,128)}, f32[384,3072]{1,0:T(8,128)}, f32[1536,768]{1,0:T(8,128)}) async-done(((f32[384,2304]{1,0:T(8,128)}, f32[384,768]{1,0:T(8,128)}, f32[384,3072]{1,0:T(8,128)}, f32[1536,768]{1,0:T(8,128)}), (f32[384,2304]{1,0:T(8,128)}, f32[384,768]{1,0:T(8,128)}, f32[384,3072]{1,0:T(8,128)}, ...) | async-done | bytes 14155792 | tf_op jit(solution)/shard_map/psum | solution.py:243
  (780 shorter events, 413.7 us)
Async XLA Ops:
  7.2 17.8 %all-gather.13.cloned.1.call-start = ((), (), s32[]{:S(2)}) async-start(), calls=%async_computation.8 | async-start | bytes 5308416 | tf_op jit(solution)/shard_map/all_gather | solution.py:131
  7.9 82.5 %all-gather.25.cloned.1.call-start = ((), (), s32[]{:S(2)}) async-start(), calls=%async_computation.14 | async-start | bytes 3538944 | tf_op jit(solution)/shard_map/all_gather | solution.py:165
  29.1 122.8 %all-gather.27.cloned.1.call-start = ((), (), s32[]{:S(2)}) async-start(), calls=%async_computation.15 | async-start | bytes 3538944 | tf_op jit(solution)/shard_map/all_gather | solution.py:164
  51.8 154.7 %all-gather.19.cloned.1.call-start = ((), (), s32[]{:S(2)}) async-start(), calls=%async_computation.11 | async-start | bytes 1769472 | tf_op jit(solution)/shard_map/all_gather | solution.py:134
  52.4 172.1 %all-gather.15.cloned.1.call-start = ((), (), s32[]{:S(2)}) async-start(), calls=%async_computation.9 | async-start | bytes 3538944 | tf_op jit(solution)/shard_map/all_gather | solution.py:165
  54.5 231.4 %all-gather.17.cloned.1.call-start = ((), (), s32[]{:S(2)}) async-start(), calls=%async_computation.10 | async-start | bytes 3538944 | tf_op jit(solution)/shard_map/all_gather | solution.py:164
  55.0 284.3 %all-gather.21.cloned.1.call-start = ((), (), s32[]{:S(2)}) async-start(), calls=%async_computation.12 | async-start | bytes 7077888 | tf_op jit(solution)/shard_map/all_gather | solution.py:137
  55.8 307.4 %all-gather.23.cloned.1.call-start = ((), (), s32[]{:S(2)}) async-start(), calls=%async_computation.13 | async-start | bytes 7077888 | tf_op jit(solution)/shard_map/all_gather | solution.py:138
  56.6 542.8 %reduce-scatter.13.cloned.1.call-start = ((), (), s32[]{:S(2)}) async-start(), calls=%async_computation.18 | async-start | bytes 3538944 | tf_op jit(solution)/shard_map/reduce_scatter | solution.py:206
  65.2 30.0 %copy-start.100 = (f32[256,6,2]{0,2,1:T(2,128)}, f32[256,6,2]{0,2,1:T(2,128)S(1)}, u32[]{:S(2)}) copy-start(f32[256,6,2]{0,2,1:T(2,128)S(1)} %rsqrt.97) | copy-start | bytes 36868
  65.5 29.8 %copy-start.5 = (f32[1,256,768]{1,2,0:T(8,128)}, f32[1,256,768]{1,2,0:T(8,128)S(1)}, u32[]{:S(2)}) copy-start(f32[1,256,768]{1,2,0:T(8,128)S(1)} %copy.198) | copy-start | bytes 2359300
  65.6 29.7 %copy-start.73 = (f32[256,12]{0,1:T(8,128)}, f32[256,12]{0,1:T(8,128)S(1)}, u32[]{:S(2)}) copy-start(f32[256,12]{0,1:T(8,128)S(1)} %broadcast_multiply_fusion.1) | copy-start | bytes 36868
  65.6 29.6 %copy-start.102 = (f32[256,6,2]{0,2,1:T(2,128)}, f32[256,6,2]{0,2,1:T(2,128)S(1)}, u32[]{:S(2)}) copy-start(f32[256,6,2]{0,2,1:T(2,128)S(1)} %div.200) | copy-start | bytes 36868
  65.7 29.5 %copy-start.94 = (f32[256,12]{0,1:T(8,128)}, f32[256,12]{0,1:T(8,128)S(1)}, u32[]{:S(2)}) copy-start(f32[256,12]{0,1:T(8,128)S(1)} %multiply_reduce_fusion.14) | copy-start | bytes 36868
  65.8 29.5 %copy-start.108 = (f32[256,6,2]{0,2,1:T(2,128)}, f32[256,6,2]{0,2,1:T(2,128)S(1)}, u32[]{:S(2)}) copy-start(f32[256,6,2]{0,2,1:T(2,128)S(1)} %add.307) | copy-start | bytes 36868
  65.8 29.5 %copy-start.104 = (f32[256,6,2]{0,2,1:T(2,128)}, f32[256,6,2]{0,2,1:T(2,128)S(1)}, u32[]{:S(2)}) copy-start(f32[256,6,2]{0,2,1:T(2,128)S(1)} %rsqrt.101) | copy-start | bytes 36868
  471.3 149.9 %reduce-scatter.9.cloned.1.call-start = ((), (), s32[]{:S(2)}) async-start(), calls=%async_computation.16 | async-start | bytes 3538944 | tf_op jit(solution)/shard_map/reduce_scatter | solution.py:206
  546.2 152.7 %reduce-scatter.11.cloned.1.call-start = ((), (), s32[]{:S(2)}) async-start(), calls=%async_computation.17 | async-start | bytes 3538944 | tf_op jit(solution)/shard_map/reduce_scatter | solution.py:209
  550.9 225.8 %reduce-scatter.15.cloned.1.call-start = ((), (), s32[]{:S(2)}) async-start(), calls=%async_computation.19 | async-start | bytes 3538944 | tf_op jit(solution)/shard_map/reduce_scatter | solution.py:209
  555.6 233.2 %reduce-scatter.19.cloned.1.call-start = ((), (), s32[]{:S(2)}) async-start(), calls=%async_computation.21 | async-start | bytes 3538944 | tf_op jit(solution)/shard_map/reduce_scatter | solution.py:242
  559.5 250.0 %reduce-scatter.21.cloned.1.call-start = ((), (), s32[]{:S(2)}) async-start(), calls=%async_computation.22 | async-start | bytes 14155776 | tf_op jit(solution)/shard_map/reduce_scatter | solution.py:242
  568.1 262.1 %reduce-scatter.23.cloned.1.call-start = ((), (), s32[]{:S(2)}) async-start(), calls=%async_computation.23 | async-start | bytes 14155776 | tf_op jit(solution)/shard_map/reduce_scatter | solution.py:242
  577.5 272.0 %reduce-scatter.17.cloned.1.call-start = ((), (), s32[]{:S(2)}) async-start(), calls=%async_computation.20 | async-start | bytes 10616832 | tf_op jit(solution)/shard_map/reduce_scatter | solution.py:242
  598.2 26.5 %copy-start.85 = (f32[256,12]{0,1:T(8,128)S(1)}, f32[256,12]{0,1:T(8,128)}, u32[]{:S(2)}) copy-start(f32[256,12]{0,1:T(8,128)} %copy-done.84) | copy-start | bytes 36868
  631.6 67.3 %copy-start.2 = (bf16[2,1,256,768]{3,2,1,0:T(8,128)(2,1)S(1)}, bf16[2,1,256,768]{3,2,1,0:T(8,128)(2,1)}, u32[]{:S(2)}) copy-start(bf16[2,1,256,768]{3,2,1,0:T(8,128)(2,1)} %param.21) | copy-start | bytes 2359300
  631.6 67.3 %copy-start.64 = (f32[768]{0:T(1024)S(1)}, f32[768]{0:T(1024)}, u32[]{:S(2)}) copy-start(f32[768]{0:T(1024)} %copy-done.63) | copy-start | bytes 9220
  631.7 67.3 %copy-start.66 = (f32[768]{0:T(1024)S(1)}, f32[768]{0:T(1024)}, u32[]{:S(2)}) copy-start(f32[768]{0:T(1024)} %copy-done.65) | copy-start | bytes 9220
  631.7 67.3 %copy-start.113 = (f32[256]{0:T(256)S(1)}, f32[256]{0:T(256)}, u32[]{:S(2)}) copy-start(f32[256]{0:T(256)} %copy-done.112) | copy-start | bytes 3076
  784.1 466.5 %all-reduce.14.cloned.1.call-start = ((), (), s32[]{:S(2)}) async-start(), calls=%async_computation.24 | async-start | bytes 28311552 | tf_op jit(solution)/shard_map/psum | solution.py:243
  866.6 55.5 %copy-start.28 = (bf16[2,1,256,768]{3,2,1,0:T(8,128)(2,1)S(1)}, bf16[2,1,256,768]{3,2,1,0:T(8,128)(2,1)}, u32[]{:S(2)}) copy-start(bf16[2,1,256,768]{3,2,1,0:T(8,128)(2,1)} %param.33) | copy-start | bytes 2359300
  866.6 55.4 %copy-start.30 = (f32[256,768]{1,0:T(8,128)S(1)}, f32[256,768]{1,0:T(8,128)}, u32[]{:S(2)}) copy-start(f32[256,768]{1,0:T(8,128)} %copy-done.29) | copy-start | bytes 2359300
  866.6 55.4 %copy-start.32 = (f32[256,768]{1,0:T(8,128)S(1)}, f32[256,768]{1,0:T(8,128)}, u32[]{:S(2)}) copy-start(f32[256,768]{1,0:T(8,128)} %copy-done.31) | copy-start | bytes 2359300
  (173 other events, 964.4 us)
Sparse Core Ops, SparseCore 0:
  9.5 15.4 all-gather.12
  29.2 61.1 all-gather.24
  93.2 58.6 all-gather.26
  153.3 7.8 all-gather.18
  163.2 61.2 all-gather.14
  227.1 58.6 all-gather.16
  287.4 13.0 all-gather.20
  302.0 15.6 all-gather.22
  471.4 73.0 reduce-scatter.12
  547.9 73.2 reduce-scatter.8
  625.4 73.4 reduce-scatter.10
  702.9 73.7 reduce-scatter.14
  779.6 9.2 reduce-scatter.18
  791.0 18.5 reduce-scatter.20
  811.6 18.5 reduce-scatter.22
  832.4 17.0 reduce-scatter.16
  855.8 394.8 all-reduce.13
where the time goes:
time: 1280 us; the launch traced here: 1270 us
  waiting for transfers between devices  706 us (55%)
  matrix products  268 us (21%)
  local copies, waits for them, and re-layouts  131 us (10%)
  other arithmetic  81.9 us (6%)
  blocking collectives  61.2 us (5%)
  between operations  18.8 us (1%)
    psum x1, waiting for transfers between devices, on_device(): running = lax.psum(owned, ('rep', 'seq'))  325 us
    reduce_scatter x2, waiting for transfers between devices, on_device(): lax.psum_scatter(join_groups(grad_vg).astype(jnp.bfloat16), 'seq', scatte...  132 us
    all_gather x2, waiting for transfers between devices, on_device(): lax.all_gather(keys, 'seq', axis=1, tiled=True)  113 us
    reduce_scatter x4, waiting for transfers between devices, on_device(): owned = lax.psum_scatter(running, 'fsdp', scatter_dimension=0, tiled=True)  65 us
    psum x1, blocking collectives, on_device(): running = lax.psum(owned, ('rep', 'seq'))  47.1 us
    dot_general x24, matrix products, group_scores(): jnp.einsum('rqhd,rkhd->rhqk', q_group, k_group, preferred_element_type=jn...  46.2 us
    all_gather x2, waiting for transfers between devices, on_device(): lax.all_gather(values, 'seq', axis=1, tiled=True)  36.9 us
    dot_general x12, matrix products, attend_group(): jnp.einsum('rhqk,rkhd->rqhd', probs, v_group, preferred_element_type=jnp....  35.5 us
  transfers between devices with their start and end apart: 17, of which 13 were waited for; matrix products, arithmetic and copies ran while one was open for 27% of the time, Pallas kernels for 0%

commit v1 on v0

--- a/solution.py
+++ b/solution.py
@@ -7,6 +7,31 @@
 H = 12
 EPS = 1e-06
 MASKED = -1000000000.0
+
+
+def map_leaves_on_mesh(q_in, axis_no):
+    q_in = jnp.moveaxis(q_in, 0, axis_no)
+    mid_arr = q_in.shape
+    raw_out = q_in.reshape(
+        *mid_arr[:axis_no], mid_arr[axis_no] * mid_arr[axis_no + 1], *mid_arr[axis_no + 2 :]
+    )
+    return raw_out
+
+
+def _meet_array(array_here, dev_axis):
+    outcome_arr = lax.axis_size(dev_axis)
+    r2 = lax.axis_index(dev_axis)
+    z, known = (outcome_arr, r2)
+    x_now, b_next = (array_here[None], 1)
+    while b_next < z:
+        y2 = tuple(((d, d ^ b_next) for d in range(z)))
+        response = lax.ppermute(x_now, dev_axis, y2)
+        answer = known & b_next == 0
+        u_next = jnp.where(answer, x_now, response)
+        v_now = jnp.where(answer, response, x_now)
+        x_now = jnp.concatenate([u_next, v_now])
+        b_next *= 2
+    return x_now
 
 
 def layer_norm(values, gain, shift):
@@ -160,9 +185,15 @@
         queries = q_normed.astype(jnp.bfloat16).reshape(rows, local, width)
         keys = k_normed.astype(jnp.bfloat16).reshape(rows, local, width)
         values = qkv[..., 2 * width :].astype(jnp.bfloat16)
+
+        def see_the_leaf(local_values, row_data, along_dim=1):
+            v_next = _meet_array(local_values, row_data)
+            local_out = map_leaves_on_mesh(v_next, along_dim)
+            return local_out
+
         keys_all, values_all = (
             lax.all_gather(keys, "seq", axis=1, tiled=True),
-            lax.all_gather(values, "seq", axis=1, tiled=True),
+            see_the_leaf(values, "seq"),
         )
         q_groups = split_groups(queries)
         k_groups = split_groups(keys_all)

time: 1280 us -> 1360 us (1.062)
  waiting for transfers between devices: 706 us -> 746 us
  local copies, waits for them, and re-layouts: 131 us -> 151 us
    ppermute x0 -> x6, waiting for transfers between devices: none -> 197 us  [_meet_array(): response = lax.ppermute(x_now, dev_axis, y2)]
    all_gather x2, waiting for transfers between devices: 113 us -> 0.01 us  [on_device(): lax.all_gather(keys, 'seq', axis=1, tiled=True)]
    all_gather x2 -> x0, waiting for transfers between devices: 36.9 us -> none  [on_device(): lax.all_gather(values, 'seq', axis=1, tiled=True)]
    unnamed x369 -> x363, local copies, waits for them, and re-layouts: 31.3 us -> 35.8 us
  transfers between devices with their start and end apart: 17 -> 21, of which waited for: 13 -> 15; matrix products, arithmetic and copies ran while one was open for 27% -> 27% of each run, Pallas kernels for 0% -> 0%
where the time goes in v1:
time: 1360 us; the launch traced here: 1350 us
  waiting for transfers between devices  746 us (55%)
  matrix products  268 us (20%)
  local copies, waits for them, and re-layouts  151 us (11%)
  other arithmetic  94.7 us (7%)
  blocking collectives  61.7 us (5%)
  between operations  18.7 us (1%)
    psum x1, waiting for transfers between devices, on_device(): running = lax.psum(owned, ('rep', 'seq'))  325 us
    ppermute x6, waiting for transfers between devices, _meet_array(): response = lax.ppermute(x_now, dev_axis, y2)  197 us
    reduce_scatter x2, waiting for transfers between devices, on_device(): lax.psum_scatter(join_groups(grad_vg).astype(jnp.bfloat16), 'seq', scatte...  131 us
    reduce_scatter x4, waiting for transfers between devices, on_device(): owned = lax.psum_scatter(running, 'fsdp', scatter_dimension=0, tiled=True)  65.1 us
    psum x1, blocking collectives, on_device(): running = lax.psum(owned, ('rep', 'seq'))  47.1 us
    dot_general x24, matrix products, group_scores(): jnp.einsum('rqhd,rkhd->rhqk', q_group, k_group, preferred_element_type=jn...  46.2 us
    unnamed x363, local copies, waits for them, and re-layouts  35.8 us
    dot_general x12, matrix products, attend_group(): jnp.einsum('rhqk,rkhd->rqhd', probs, v_group, preferred_element_type=jnp....  35.3 us
  transfers between devices with their start and end apart: 21, of which 15 were waited for; matrix products, arithmetic and copies ran while one was open for 27% of the time, Pallas kernels for 0%

profile of v1, /device:TPU:0, one launch (start us, length us, event | category | flops | bytes accessed | tf_op | source)
XLA Modules:
  0.0 1348.3 jit_solution(1112840923881391249)
XLA Ops:
  62.2 7.6 collective-permute-done.3
  82.2 27.7 %collective-permute-done.4 = bf16[2,1,256,768]{3,2,1,0:T(8,128)(2,1)} collective-permute-done((bf16[2,1,256,768]{3,2,1,0:T(8,128)(2,1)S(1)}, bf16[2,1,256,768]{3,2,1,0:T(8,128)(2,1)}, u32[]{:S(2)}, u32[]{:S(2)}) %collective-permute-start.4) | collective-permute-done | bytes 786464 | tf_op jit(solution)/shard_map/ppermute | solution.py:28
  113.8 39.4 %collective-permute-done.1 = bf16[2,1,256,768]{3,2,1,0:T(8,128)(2,1)} collective-permute-done((bf16[2,1,256,768]{3,2,1,0:T(8,128)(2,1)}, bf16[2,1,256,768]{3,2,1,0:T(8,128)(2,1)}, u32[]{:S(2)}, u32[]{:S(2)}) %collective-permute-start.1) | collective-permute-done | bytes 786464 | tf_op jit(solution)/shard_map/ppermute | solution.py:28
  162.3 99.8 %collective-permute-done.5 = bf16[4,1,256,768]{3,2,1,0:T(8,128)(2,1)} collective-permute-done((bf16[4,1,256,768]{3,2,1,0:T(8,128)(2,1)}, bf16[4,1,256,768]{3,2,1,0:T(8,128)(2,1)}, u32[]{:S(2)}, u32[]{:S(2)}) %collective-permute-start.5) | collective-permute-done | bytes 1572896 | tf_op jit(solution)/shard_map/ppermute | solution.py:28
  267.5 6.0 reshape_reshape_transpose.7
  273.5 21.3 %collective-permute-done.2 = bf16[4,1,256,768]{3,2,1,0:T(8,128)(2,1)} collective-permute-done((bf16[4,1,256,768]{3,2,1,0:T(8,128)(2,1)}, bf16[4,1,256,768]{3,2,1,0:T(8,128)(2,1)}, u32[]{:S(2)}, u32[]{:S(2)}) %collective-permute-start.2) | collective-permute-done | bytes 1572896 | tf_op jit(solution)/shard_map/ppermute | solution.py:28
  300.2 5.9 reshape_reshape_transpose.6
  310.9 46.9 %while.57 = (s32[]{:T(128)}, f32[6,1,256,2,64]{2,4,3,1,0:T(8,128)}, f32[6,1,2,256]{3,2,1,0:T(2,128)}, bf16[6,1,2048,2,64]{2,4,3,1,0:T(8,128)(2,1)}, bf16[6,1,256...) while((s32[]{:T(128)}, f32[6,1,256,2,64]{2,4,3,1,0:T(8,128)}, ...), condition=%wide.region_25.26_spmd.clone, body=%wide.region_22.25_spmd.clone.sunk | while | flops 282066432 | bytes 15955057 | solution.py:201
  369.9 41.9 %while.56 = (s32[]{:T(128)}, f32[6,1,256,2,64]{2,4,3,1,0:T(8,128)}, f32[6,1,2,256]{3,2,1,0:T(2,128)}, bf16[6,1,2048,2,64]{2,4,3,1,0:T(8,128)(2,1)}, bf16[6,1,256...) while((s32[]{:T(128)}, f32[6,1,256,2,64]{2,4,3,1,0:T(8,128)}, ...), condition=%wide.region_11.12_spmd.clone, body=%wide.region_8.11_spmd.clone.sunk | while | flops 282066432 | bytes 15955057 | solution.py:201
  418.6 11.7 multiply_convert_fusion.2
  430.4 11.4 multiply_convert_fusion.3
  441.8 6.4 add_convert_fusion
  467.3 77.8 %while.59 = (s32[]{:T(128)}, f32[6,1,256,2,64]{2,4,3,1,0:T(8,128)}, bf16[6,1,2048,2,64]{2,4,3,1,0:T(8,128)(2,1)}, bf16[6,1,2048,2,64]{2,4,3,1,0:T(8,128)(2,1)}, ...) while((s32[]{:T(128)}, f32[6,1,256,2,64]{2,4,3,1,0:T(8,128)}, ...), condition=%wide.region_45.46_spmd.clone, body=%wide.region_43.45_spmd.clone.sunk | while | flops 681868800 | bytes 36608192 | solution.py:232
  545.1 4.6 copy.242
  560.2 59.9 %while.58 = (s32[]{:T(128)}, f32[6,1,256,2,64]{2,4,3,1,0:T(8,128)}, bf16[6,1,2048,2,64]{2,4,3,1,0:T(8,128)(2,1)}, bf16[6,1,2048,2,64]{2,4,3,1,0:T(8,128)(2,1)}, ...) while((s32[]{:T(128)}, f32[6,1,256,2,64]{2,4,3,1,0:T(8,128)}, ...), condition=%wide.region_32.33_spmd.clone, body=%wide.region_30.32_spmd.clone.sunk | while | flops 681868800 | bytes 36595848 | solution.py:232
  620.1 4.7 copy.223
  641.5 5.3 convolution_add_fusion.2
  650.9 5.1 convolution_add_fusion.1
  679.2 22.6 %reduce-scatter.9.cloned.1.call-done = bf16[1,256,768]{2,1,0:T(8,128)(2,1)} async-done(((bf16[1,2048,768]{2,1,0:T(8,128)(2,1)}), bf16[1,256,768]{2,1,0:T(8,128)(2,1)}) %reduce-scatter.9.cloned.1.call-update) | async-done | bytes 393232 | tf_op jit(solution)/shard_map/reduce_scatter | solution.py:237
  712.2 5.0 multiply_reduce_fusion.5
  717.2 61.7 %reduce-scatter.11.cloned.1.call-done = bf16[1,256,768]{2,1,0:T(8,128)(2,1)} async-done(((bf16[1,2048,768]{2,1,0:T(8,128)(2,1)}), bf16[1,256,768]{2,1,0:T(8,128)(2,1)}) %reduce-scatter.11.cloned.1.call-update) | async-done | bytes 393232 | tf_op jit(solution)/shard_map/reduce_scatter | solution.py:240
  779.0 5.5 fusion.159
  787.1 69.3 %reduce-scatter.15.cloned.1.call-done = bf16[1,256,768]{2,1,0:T(8,128)(2,1)} async-done(((bf16[1,2048,768]{2,1,0:T(8,128)(2,1)}), bf16[1,256,768]{2,1,0:T(8,128)(2,1)}) %reduce-scatter.15.cloned.1.call-update) | async-done | bytes 393232 | tf_op jit(solution)/shard_map/reduce_scatter | solution.py:240
  856.4 7.4 convolution_add_fusion
  864.1 4.3 reduce-scatter.19.cloned.1.call-done
  868.4 20.7 %reduce-scatter.21.cloned.1.call-done = f32[384,3072]{1,0:T(8,128)} async-done(((f32[768,3072]{1,0:T(8,128)}), f32[384,3072]{1,0:T(8,128)}) %reduce-scatter.21.cloned.1.call-update) | async-done | bytes 4718608 | tf_op jit(solution)/shard_map/reduce_scatter | solution.py:273
  889.1 20.8 %reduce-scatter.23.cloned.1.call-done = f32[1536,768]{1,0:T(8,128)} async-done(((f32[3072,768]{1,0:T(8,128)}), f32[1536,768]{1,0:T(8,128)}) %reduce-scatter.23.cloned.1.call-update) | async-done | bytes 4718608 | tf_op jit(solution)/shard_map/reduce_scatter | solution.py:273
  910.0 19.3 %reduce-scatter.17.cloned.1.call-done = f32[384,2304]{1,0:T(8,128)} async-done(((f32[768,2304]{1,0:T(8,128)}), f32[384,2304]{1,0:T(8,128)}) %reduce-scatter.17.cloned.1.call-update) | async-done | bytes 3538960 | tf_op jit(solution)/shard_map/reduce_scatter | solution.py:273
  932.3 4.3 fusion.110
  954.6 47.1 %all-reduce.8 = (f32[384]{0:T(512)}, f32[384]{0:T(512)}, f32[32]{0:T(128)}, f32[32]{0:T(128)}, f32[384]{0:T(512)}, /*index=5*/f32[384]{0:T(512)}) all-reduce(f32[384]{0:T(512)S(1)} %dynamic-slice.3, f32[384]{0:T(512)S(1)} %dynamic-slice.5, f32[32]{0:T(128)S(1)} %dynamic-slice.7, ...), channel_id=1, replica_groups=mesh['rep'=2,'fsdp'=2,'seq'=8] {'rep','seq'}, use_global_device_ids=true, to_apply=%region_57.58 | all-reduce | flops 1600 | bytes 12800 | tf_op jit(solution)/shard_map/psum | solution.py:274
  1005.2 325.2 %all-reduce.14.cloned.1.call-done = (f32[384,2304]{1,0:T(8,128)}, f32[384,768]{1,0:T(8,128)}, f32[384,3072]{1,0:T(8,128)}, f32[1536,768]{1,0:T(8,128)}) async-done(((f32[384,2304]{1,0:T(8,128)}, f32[384,768]{1,0:T(8,128)}, f32[384,3072]{1,0:T(8,128)}, f32[1536,768]{1,0:T(8,128)}), (f32[384,2304]{1,0:T(8,128)}, f32[384,768]{1,0:T(8,128)}, f32[384,3072]{1,0:T(8,128)}, ...) | async-done | bytes 14155792 | tf_op jit(solution)/shard_map/psum | solution.py:274
  1330.4 4.2 copy.314
  (793 shorter events, 454.6 us)
Async XLA Ops:
  7.2 17.8 %all-gather.11.cloned.1.call-start = ((), (), s32[]{:S(2)}) async-start(), calls=%async_computation.8 | async-start | bytes 5308416 | tf_op jit(solution)/shard_map/all_gather | solution.py:156
  7.9 298.2 %all-gather.21.cloned.1.call-start = ((), (), s32[]{:S(2)}) async-start(), calls=%async_computation.13 | async-start | bytes 3538944 | tf_op jit(solution)/shard_map/all_gather | solution.py:195
  50.0 310.6 %all-gather.15.cloned.1.call-start = ((), (), s32[]{:S(2)}) async-start(), calls=%async_computation.10 | async-start | bytes 1769472 | tf_op jit(solution)/shard_map/all_gather | solution.py:159
  50.7 314.3 %all-gather.13.cloned.1.call-start = ((), (), s32[]{:S(2)}) async-start(), calls=%async_computation.9 | async-start | bytes 3538944 | tf_op jit(solution)/shard_map/all_gather | solution.py:195
  51.3 367.2 %all-gather.17.cloned.1.call-start = ((), (), s32[]{:S(2)}) async-start(), calls=%async_computation.11 | async-start | bytes 7077888 | tf_op jit(solution)/shard_map/all_gather | solution.py:162
  51.9 389.9 %all-gather.19.cloned.1.call-start = ((), (), s32[]{:S(2)}) async-start(), calls=%async_computation.12 | async-start | bytes 7077888 | tf_op jit(solution)/shard_map/all_gather | solution.py:163
  52.5 625.5 %reduce-scatter.13.cloned.1.call-start = ((), (), s32[]{:S(2)}) async-start(), calls=%async_computation.16 | async-start | bytes 3538944 | tf_op jit(solution)/shard_map/reduce_scatter | solution.py:237
  53.9 15.9 %collective-permute-start.3 = (bf16[1,1,256,768]{3,2,1,0:T(8,128)(2,1)S(1)}, bf16[1,1,256,768]{3,2,1,0:T(8,128)(2,1)S(1)}, u32[]{:S(2)}, u32[]{:S(2)}) collective-permute-start(bf16[1,1,256,768]{3,2,1,0:T(8,128)(2,1)S(1)} %fusion.164), channel_id=1, source_target_pairs={{0,1},{1,0},{2,3},{3,2},{4,5},{5,4},{6,7},{7,6},{8,9},{9,8},{10,11... | collective-permute-start | bytes 1179656 | tf_op jit(solution)/shard_map/ppermute | solution.py:28
  61.9 16.1 %collective-permute-start = (bf16[1,1,256,768]{3,2,1,0:T(8,128)(2,1)}, bf16[1,1,256,768]{3,2,1,0:T(8,128)(2,1)}, u32[]{:S(2)}, u32[]{:S(2)}) collective-permute-start(bf16[1,1,256,768]{3,2,1,0:T(8,128)(2,1)} %fusion.163), channel_id=1, source_target_pairs={{0,1},{1,0},{2,3},{3,2},{4,5},{5,4},{6,7},{7,6},{8,9},{9,8},{10,11... | collective-permute-start | bytes 1179656 | tf_op jit(solution)/shard_map/ppermute | solution.py:28
  70.7 39.1 %collective-permute-start.4 = (bf16[2,1,256,768]{3,2,1,0:T(8,128)(2,1)S(1)}, bf16[2,1,256,768]{3,2,1,0:T(8,128)(2,1)}, u32[]{:S(2)}, u32[]{:S(2)}) collective-permute-start(bf16[2,1,256,768]{3,2,1,0:T(8,128)(2,1)S(1)} %pad_maximum_fusion.8), channel_id=1, source_target_pairs={{0,2},{1,3},{2,0},{3,1},{4,6},{5,7},{6,4},{7,5},{8,10},{9,11},{10,... | collective-permute-start | bytes 2359304 | tf_op jit(solution)/shard_map/ppermute | solution.py:28
  76.7 83.6 %copy-start.3 = (f32[1,256,768]{1,2,0:T(8,128)}, f32[1,256,768]{1,2,0:T(8,128)S(1)}, u32[]{:S(2)}) copy-start(f32[1,256,768]{1,2,0:T(8,128)S(1)} %copy.184) | copy-start | bytes 2359300
  80.4 72.8 %collective-permute-start.1 = (bf16[2,1,256,768]{3,2,1,0:T(8,128)(2,1)}, bf16[2,1,256,768]{3,2,1,0:T(8,128)(2,1)}, u32[]{:S(2)}, u32[]{:S(2)}) collective-permute-start(bf16[2,1,256,768]{3,2,1,0:T(8,128)(2,1)} %pad_maximum_fusion.7), channel_id=1, source_target_pairs={{0,2},{1,3},{2,0},{3,1},{4,6},{5,7},{6,4},{7,5},{8,10},{9,11},{10,... | collective-permute-start | bytes 2359304 | tf_op jit(solution)/shard_map/ppermute | solution.py:28
  111.1 42.1 %copy-start.49 = (bf16[1,1,256,768]{3,2,1,0:T(8,128)(2,1)S(1)}, bf16[1,1,256,768]{3,2,1,0:T(8,128)(2,1)}, u32[]{:S(2)}) copy-start(bf16[1,1,256,768]{3,2,1,0:T(8,128)(2,1)} %copy-done.48) | copy-start | bytes 1179652
  112.4 149.7 %collective-permute-start.5 = (bf16[4,1,256,768]{3,2,1,0:T(8,128)(2,1)}, bf16[4,1,256,768]{3,2,1,0:T(8,128)(2,1)}, u32[]{:S(2)}, u32[]{:S(2)}) collective-permute-start(bf16[4,1,256,768]{3,2,1,0:T(8,128)(2,1)} %pad_maximum_fusion.3), channel_id=1, source_target_pairs={{0,4},{1,5},{2,6},{3,7},{4,0},{5,1},{6,2},{7,3},{8,12},{9,13},{10,... | collective-permute-start | bytes 4718600 | tf_op jit(solution)/shard_map/ppermute | solution.py:28
  112.5 44.1 %copy-start.96 = (f32[256,12]{0,1:T(8,128)}, f32[256,12]{0,1:T(8,128)S(1)}, u32[]{:S(2)}) copy-start(f32[256,12]{0,1:T(8,128)S(1)} %multiply_reduce_fusion.17) | copy-start | bytes 36868
  156.6 138.1 %collective-permute-start.2 = (bf16[4,1,256,768]{3,2,1,0:T(8,128)(2,1)}, bf16[4,1,256,768]{3,2,1,0:T(8,128)(2,1)}, u32[]{:S(2)}, u32[]{:S(2)}) collective-permute-start(bf16[4,1,256,768]{3,2,1,0:T(8,128)(2,1)} %pad_maximum_fusion.2), channel_id=1, source_target_pairs={{0,4},{1,5},{2,6},{3,7},{4,0},{5,1},{6,2},{7,3},{8,12},{9,13},{10,... | collective-permute-start | bytes 4718600 | tf_op jit(solution)/shard_map/ppermute | solution.py:28
  158.7 105.0 %copy-start.5 = (f32[1,256,768]{1,2,0:T(8,128)}, f32[1,256,768]{1,2,0:T(8,128)S(1)}, u32[]{:S(2)}) copy-start(f32[1,256,768]{1,2,0:T(8,128)S(1)} %copy.198) | copy-start | bytes 2359300
  549.8 152.0 %reduce-scatter.9.cloned.1.call-start = ((), (), s32[]{:S(2)}) async-start(), calls=%async_computation.14 | async-start | bytes 3538944 | tf_op jit(solution)/shard_map/reduce_scatter | solution.py:237
  624.8 154.0 %reduce-scatter.11.cloned.1.call-start = ((), (), s32[]{:S(2)}) async-start(), calls=%async_computation.15 | async-start | bytes 3538944 | tf_op jit(solution)/shard_map/reduce_scatter | solution.py:240
  629.5 226.8 %reduce-scatter.15.cloned.1.call-start = ((), (), s32[]{:S(2)}) async-start(), calls=%async_computation.17 | async-start | bytes 3538944 | tf_op jit(solution)/shard_map/reduce_scatter | solution.py:240
  634.3 234.2 %reduce-scatter.19.cloned.1.call-start = ((), (), s32[]{:S(2)}) async-start(), calls=%async_computation.19 | async-start | bytes 3538944 | tf_op jit(solution)/shard_map/reduce_scatter | solution.py:273
  638.2 250.9 %reduce-scatter.21.cloned.1.call-start = ((), (), s32[]{:S(2)}) async-start(), calls=%async_computation.20 | async-start | bytes 14155776 | tf_op jit(solution)/shard_map/reduce_scatter | solution.py:273
  646.8 263.2 %reduce-scatter.23.cloned.1.call-start = ((), (), s32[]{:S(2)}) async-start(), calls=%async_computation.21 | async-start | bytes 14155776 | tf_op jit(solution)/shard_map/reduce_scatter | solution.py:273
  656.1 273.1 %reduce-scatter.17.cloned.1.call-start = ((), (), s32[]{:S(2)}) async-start(), calls=%async_computation.18 | async-start | bytes 10616832 | tf_op jit(solution)/shard_map/reduce_scatter | solution.py:273
  712.1 66.7 %copy-start.2 = (bf16[2,1,256,768]{3,2,1,0:T(8,128)(2,1)S(1)}, bf16[2,1,256,768]{3,2,1,0:T(8,128)(2,1)}, u32[]{:S(2)}) copy-start(bf16[2,1,256,768]{3,2,1,0:T(8,128)(2,1)} %param.21) | copy-start | bytes 2359300
  712.1 66.7 %copy-start.68 = (f32[768]{0:T(1024)S(1)}, f32[768]{0:T(1024)}, u32[]{:S(2)}) copy-start(f32[768]{0:T(1024)} %copy-done.67) | copy-start | bytes 9220
  712.1 66.7 %copy-start.70 = (f32[768]{0:T(1024)S(1)}, f32[768]{0:T(1024)}, u32[]{:S(2)}) copy-start(f32[768]{0:T(1024)} %copy-done.69) | copy-start | bytes 9220
  712.2 66.7 %copy-start.114 = (f32[256]{0:T(256)S(1)}, f32[256]{0:T(256)}, u32[]{:S(2)}) copy-start(f32[256]{0:T(256)} %copy-done.113) | copy-start | bytes 3076
  863.8 466.6 %all-reduce.14.cloned.1.call-start = ((), (), s32[]{:S(2)}) async-start(), calls=%async_computation.22 | async-start | bytes 28311552 | tf_op jit(solution)/shard_map/psum | solution.py:274
  946.3 55.5 %copy-start.29 = (bf16[2,1,256,768]{3,2,1,0:T(8,128)(2,1)S(1)}, bf16[2,1,256,768]{3,2,1,0:T(8,128)(2,1)}, u32[]{:S(2)}) copy-start(bf16[2,1,256,768]{3,2,1,0:T(8,128)(2,1)} %param.33) | copy-start | bytes 2359300
  946.3 55.4 %copy-start.31 = (f32[256,768]{1,0:T(8,128)S(1)}, f32[256,768]{1,0:T(8,128)}, u32[]{:S(2)}) copy-start(f32[256,768]{1,0:T(8,128)} %copy-done.30) | copy-start | bytes 2359300
  946.4 55.4 %copy-start.33 = (f32[256,768]{1,0:T(8,128)S(1)}, f32[256,768]{1,0:T(8,128)}, u32[]{:S(2)}) copy-start(f32[256,768]{1,0:T(8,128)} %copy-done.32) | copy-start | bytes 2359300
  (173 other events, 1028.1 us)
Sparse Core Ops, SparseCore 0:
  9.5 15.4 all-gather.10
  50.1 95.3 all-gather.20
  147.0 7.0 all-gather.14
  156.2 113.9 all-gather.12
  271.6 13.2 all-gather.16
  286.3 15.6 all-gather.18
  549.9 74.7 reduce-scatter.12
  628.3 73.4 reduce-scatter.8
  705.3 73.4 reduce-scatter.10
  782.9 73.4 reduce-scatter.14
  859.2 9.1 reduce-scatter.18
  870.6 18.5 reduce-scatter.20
  891.4 18.5 reduce-scatter.22
  912.1 17.0 reduce-scatter.16
  935.5 394.8 all-reduce.13
